TPU v7x, 128 devices: a whole 4x4x4 slice. The times are simulated.
128 devices in a mesh: gx: 8 (over y_hi, x), gy: 4 (over z), gz: 4 (over y_lo, core).
Axes of the slice: x: 4, y: 4 (y_hi: 2, y_lo: 2; y = y_hi * 2 + y_lo), z: 4, core: 2. Of those that a mesh axis runs over, the one named last changes fastest.
Arguments:
- coeffs: float32 [128, 512, 512], P(('gx', 'gy', 'gz')), may hold values from -6 to 6
- transfer: float32 [4, 128, 512, 1024], P(None, ('gx', 'gy', 'gz')), may hold values from -0.1875 to 0.1875
Outputs:
- result: float32 [128, 512, 512], P(('gx', 'gy', 'gz'))
All inputs are finite; a program needn't handle non-finite values.
Results may differ from a plain program's by a relative error of at most 0.0001.
Values sent between devices are 32-bit elements; how exact they have to be, the bound alone decides.
A program may use at most 64 MiB of HBM per device.

v0:
```python
import jax
import jax.numpy as jnp
from jax import lax
from jax.sharding import PartitionSpec as P

LEVELS = 4


def from_partner(block, axis, stride):
    count = lax.axis_size(axis)
    route = []
    for low in range(count):
        high = low | 1 << stride
        if high != low and high < count:
            route += [(low, high), (high, low)]
    return lax.ppermute(block, axis, route)


def apply_level(matrix, own, other, upper):
    lower_part = jnp.where(upper == 1, other, own)
    upper_part = jnp.where(upper == 1, own, other)
    stacked = jnp.concatenate([lower_part, upper_part], axis=0)
    return jnp.dot(
        matrix, stacked, precision=lax.Precision.HIGHEST, preferred_element_type=jnp.float32
    )


def per_device(coeffs, transfer):
    nbits = lax.axis_size(("gx", "gy", "gz")).bit_length() - 1
    index = lax.axis_index(("gx", "gy", "gz"))
    current = coeffs[0]
    for level in range(LEVELS):
        bit = nbits - 1 - level
        upper = index >> bit & 1
        matrix = transfer[level, 0]
        other = from_partner(current, ("gx", "gy", "gz"), bit)
        current = apply_level(matrix, current, other, upper)
    return current[None]


def solution(mesh):
    placed = (P(("gx", "gy", "gz"), None, None), P(None, ("gx", "gy", "gz"), None, None))
    return jax.shard_map(
        per_device,
        mesh=mesh,
        in_specs=placed,
        out_specs=P(("gx", "gy", "gz"), None, None),
        check_vma=False,
    )
```

profile of v0, /device:TPU:0, one launch (start us, length us, event | category | flops | bytes accessed | tf_op | source)
XLA Modules:
  0.0 127.6 jit_solution(10527596258401535594)
XLA Ops:
  0.0 3.3 %collective-permute-start = (f32[512,512]{1,0:T(8,128)}, f32[512,512]{1,0:T(8,128)S(1)}, u32[]{:S(2)}, u32[]{:S(2)}) collective-permute-start(f32[512,512]{1,0:T(8,128)} %bitcast.33), channel_id=1, source_target_pairs={{0,64},{64,0},{1,65},{65,1},{2,66},{66,2},{3,67},{67,3},{4,68},{68... | collective-permute-start | bytes 3145736 | tf_op jit(solution)/shard_map/ppermute | solution.py:16
  3.3 23.4 %collective-permute-done = f32[512,512]{1,0:T(8,128)S(1)} collective-permute-done((f32[512,512]{1,0:T(8,128)}, f32[512,512]{1,0:T(8,128)S(1)}, u32[]{:S(2)}, u32[]{:S(2)}) %collective-permute-start) | collective-permute-done | bytes 1048608 | tf_op jit(solution)/shard_map/ppermute | solution.py:16
  26.7 1.4 %broadcast_select_fusion.1 = (f32[512,512]{1,0:T(8,128)S(1)}, f32[512,512]{1,0:T(8,128)S(1)}) fusion(f32[512,512]{1,0:T(8,128)S(1)} %collective-permute-done, pred[]{:T(512)S(6)} %eq.19, f32[1,512,512]{2,1,0:T(8,128)} %param.2), kind=kLoop, calls=%fused_computation.29 | loop fusion | flops 524288 | bytes 4194305 | tf_op jit(solution)/shard_map/jit(_where)/select_n | solution.py:20
  28.1 5.1 %fusion.39 = f32[512,512]{1,0:T(8,128)S(1)} fusion(f32[4,1,512,1024]{3,2,1,0:T(8,128)} %param.3, f32[512,512]{1,0:T(8,128)S(1)} %get-tuple-element.12, f32[512,512]{1,0:T(8,128)S(1)} %get-tuple-element.11), kind=kOutput, calls=%fused_computation.27 | convolution fusion | flops 3221749760 | bytes 5242880 | tf_op jit(solution)/shard_map/dot_general | solution.py:23
  33.3 3.2 %collective-permute-start.1 = (f32[512,512]{1,0:T(8,128)S(1)}, f32[512,512]{1,0:T(8,128)S(1)}, u32[]{:S(2)}, u32[]{:S(2)}) collective-permute-start(f32[512,512]{1,0:T(8,128)S(1)} %fusion.39), channel_id=1, source_target_pairs={{0,32},{32,0},{1,33},{33,1},{2,34},{34,2},{3,35},{35,3},{4,36},{36... | collective-permute-start | bytes 3145736 | tf_op jit(solution)/shard_map/ppermute | solution.py:16
  36.4 22.5 %collective-permute-done.1 = f32[512,512]{1,0:T(8,128)S(1)} collective-permute-done((f32[512,512]{1,0:T(8,128)S(1)}, f32[512,512]{1,0:T(8,128)S(1)}, u32[]{:S(2)}, u32[]{:S(2)}) %collective-permute-start.1) | collective-permute-done | bytes 1048608 | tf_op jit(solution)/shard_map/ppermute | solution.py:16
  58.9 0.2 broadcast_select_fusion.3
  59.2 5.1 %fusion.34 = f32[512,512]{1,0:T(8,128)S(1)} fusion(f32[4,1,512,1024]{3,2,1,0:T(8,128)} %param.3, f32[512,512]{1,0:T(8,128)S(1)} %get-tuple-element.10, f32[512,512]{1,0:T(8,128)S(1)} %get-tuple-element.9), kind=kOutput, calls=%fused_computation.26 | convolution fusion | flops 3221749760 | bytes 5242880 | tf_op jit(solution)/shard_map/dot_general | solution.py:23
  64.3 1.6 %collective-permute-start.2 = (f32[512,512]{1,0:T(8,128)S(1)}, f32[512,512]{1,0:T(8,128)S(1)}, u32[]{:S(2)}, u32[]{:S(2)}) collective-permute-start(f32[512,512]{1,0:T(8,128)S(1)} %fusion.34), channel_id=1, source_target_pairs={{0,16},{16,0},{1,17},{17,1},{2,18},{18,2},{3,19},{19,3},{4,20},{20... | collective-permute-start | bytes 3145736 | tf_op jit(solution)/shard_map/ppermute | solution.py:16
  65.9 21.7 %collective-permute-done.2 = f32[512,512]{1,0:T(8,128)S(1)} collective-permute-done((f32[512,512]{1,0:T(8,128)S(1)}, f32[512,512]{1,0:T(8,128)S(1)}, u32[]{:S(2)}, u32[]{:S(2)}) %collective-permute-start.2) | collective-permute-done | bytes 1048608 | tf_op jit(solution)/shard_map/ppermute | solution.py:16
  87.6 0.2 broadcast_select_fusion.5
  87.8 5.1 %fusion.29 = f32[512,512]{1,0:T(8,128)S(1)} fusion(f32[4,1,512,1024]{3,2,1,0:T(8,128)} %param.3, f32[512,512]{1,0:T(8,128)S(1)} %get-tuple-element.8, f32[512,512]{1,0:T(8,128)S(1)} %get-tuple-element.7), kind=kOutput, calls=%fused_computation.25 | convolution fusion | flops 3221749760 | bytes 5242880 | tf_op jit(solution)/shard_map/dot_general | solution.py:23
  93.0 4.1 %collective-permute-start.3 = (f32[512,512]{1,0:T(8,128)S(1)}, f32[512,512]{1,0:T(8,128)S(1)}, u32[]{:S(2)}, u32[]{:S(2)}) collective-permute-start(f32[512,512]{1,0:T(8,128)S(1)} %fusion.29), channel_id=1, source_target_pairs={{0,8},{8,0},{1,9},{9,1},{2,10},{10,2},{3,11},{11,3},{4,12},{12,4},... | collective-permute-start | bytes 3145736 | tf_op jit(solution)/shard_map/ppermute | solution.py:16
  97.0 20.6 %collective-permute-done.3 = f32[512,512]{1,0:T(8,128)S(1)} collective-permute-done((f32[512,512]{1,0:T(8,128)S(1)}, f32[512,512]{1,0:T(8,128)S(1)}, u32[]{:S(2)}, u32[]{:S(2)}) %collective-permute-start.3) | collective-permute-done | bytes 1048608 | tf_op jit(solution)/shard_map/ppermute | solution.py:16
  117.6 0.2 broadcast_select_fusion.7
  117.9 8.5 %fusion.24 = f32[1,512,512]{1,2,0:T(8,128)S(1)} fusion(f32[4,1,512,1024]{3,2,1,0:T(8,128)} %param.3, f32[512,512]{1,0:T(8,128)S(1)} %get-tuple-element.6, f32[512,512]{1,0:T(8,128)S(1)} %get-tuple-element.5), kind=kOutput, calls=%fused_computation.24 | convolution fusion | flops 3221749760 | bytes 5242880 | tf_op jit(solution)/shard_map/dot_general | solution.py:23
  126.3 1.3 %copy.3 = f32[1,512,512]{2,1,0:T(8,128)} copy(f32[1,512,512]{1,2,0:T(8,128)S(1)} %fusion.24) | data formatting | bytes 2097152 | tf_op jit(solution)/shard_map/broadcast_in_dim | solution.py:38
Async XLA Ops:
  0.0 26.7 %collective-permute-start = (f32[512,512]{1,0:T(8,128)}, f32[512,512]{1,0:T(8,128)S(1)}, u32[]{:S(2)}, u32[]{:S(2)}) collective-permute-start(f32[512,512]{1,0:T(8,128)} %bitcast.33), channel_id=1, source_target_pairs={{0,64},{64,0},{1,65},{65,1},{2,66},{66,2},{3,67},{67,3},{4,68},{68... | collective-permute-start | bytes 3145736 | tf_op jit(solution)/shard_map/ppermute | solution.py:16
  33.3 25.7 %collective-permute-start.1 = (f32[512,512]{1,0:T(8,128)S(1)}, f32[512,512]{1,0:T(8,128)S(1)}, u32[]{:S(2)}, u32[]{:S(2)}) collective-permute-start(f32[512,512]{1,0:T(8,128)S(1)} %fusion.39), channel_id=1, source_target_pairs={{0,32},{32,0},{1,33},{33,1},{2,34},{34,2},{3,35},{35,3},{4,36},{36... | collective-permute-start | bytes 3145736 | tf_op jit(solution)/shard_map/ppermute | solution.py:16
  64.3 23.3 %collective-permute-start.2 = (f32[512,512]{1,0:T(8,128)S(1)}, f32[512,512]{1,0:T(8,128)S(1)}, u32[]{:S(2)}, u32[]{:S(2)}) collective-permute-start(f32[512,512]{1,0:T(8,128)S(1)} %fusion.34), channel_id=1, source_target_pairs={{0,16},{16,0},{1,17},{17,1},{2,18},{18,2},{3,19},{19,3},{4,20},{20... | collective-permute-start | bytes 3145736 | tf_op jit(solution)/shard_map/ppermute | solution.py:16
  93.0 24.7 %collective-permute-start.3 = (f32[512,512]{1,0:T(8,128)S(1)}, f32[512,512]{1,0:T(8,128)S(1)}, u32[]{:S(2)}, u32[]{:S(2)}) collective-permute-start(f32[512,512]{1,0:T(8,128)S(1)} %fusion.29), channel_id=1, source_target_pairs={{0,8},{8,0},{1,9},{9,1},{2,10},{10,2},{3,11},{11,3},{4,12},{12,4},... | collective-permute-start | bytes 3145736 | tf_op jit(solution)/shard_map/ppermute | solution.py:16
where the time goes:
time: 128 us
  waiting for transfers between devices  88.2 us (69%)
  matrix products  23.8 us (19%)
  starting transfers between devices  12.1 us (9%)
  other arithmetic  2.12 us (2%)
  local copies, waits for them, and re-layouts  1.31 us (1%)
    ppermute x4, waiting for transfers between devices, from_partner(): return lax.ppermute(block, axis, route)  88.2 us
    dot_general x4, matrix products, apply_level(): jnp.dot(matrix, stacked, precision=lax.Precision.HIGHEST, preferred_eleme...  23.8 us
    ppermute x4, starting transfers between devices, from_partner(): return lax.ppermute(block, axis, route)  12.1 us
  transfers between devices with their start and end apart: 4, of which 4 were waited for; matrix products, arithmetic and copies ran while one was open for 0% of the time, Pallas kernels for 0%

commit v1 on v0

v1 whole, which is shorter than its diff:
```python
import functools

import jax
import jax.numpy as jnp
from jax import lax
from jax.experimental import pallas as pl
from jax.experimental.pallas import tpu as pltpu
from jax.sharding import PartitionSpec as P

MESH = pl.DeviceIdType.MESH
LEVELS = 4
RANK = 512
BF16 = jnp.bfloat16
F32 = jnp.float32
AXES = ("gx", "gy", "gz")

CHUNKS = tuple((64 * k, 64) for k in range(8))
ORDER = (
    (0, 0), (0, 1), (0, 2), (1, 0), (0, 3), (1, 1), (0, 4), (1, 2), (2, 0), (0, 5), (0, 6), (1, 3), (2, 1), (3, 0),
    (0, 7), (1, 4), (2, 2), (3, 1), (1, 5), (3, 2), (1, 6), (2, 3), (1, 7), (2, 4), (3, 3), (2, 5), (2, 6), (3, 4),
    (2, 7), (3, 5), (3, 6), (3, 7),
)


def position(level):
    place = [lax.axis_index(a) for a in AXES]
    axis, low = ((0, 4), (0, 2), (0, 1), (1, 2))[level]
    upper = lax.rem(lax.div(place[axis], low), 2)
    place[axis] = place[axis] + low - 2 * low * upper
    return upper, tuple(place)


def split(x):
    high = x.astype(BF16)
    return high, (x - high.astype(F32)).astype(BF16)


def product(rows, high_ref, low_ref):
    high, low = split(rows)
    m = high_ref[...]
    total = jnp.dot(high, m, preferred_element_type=F32)
    total += jnp.dot(low, m, preferred_element_type=F32)
    total += jnp.dot(high, low_ref[...], preferred_element_type=F32)
    return total


def kernel(c_hbm, t_hbm, o_ref, c_in, t_in, high, low, own, other, last, c_sem, t_sem, send_sem, recv_sem):
    groups = [pltpu.make_async_copy(c_hbm.at[:, pl.ds(128 * g, 128)], c_in.at[:, pl.ds(128 * g, 128)], c_sem.at[g]) for g in range(4)]
    loads = [pltpu.make_async_copy(t_hbm.at[l], t_in.at[l], t_sem.at[l]) for l in range(LEVELS)]
    for copy in groups + loads:
        copy.start()

    spots = [position(l) for l in range(LEVELS)]
    barrier = pltpu.get_barrier_semaphore()
    for _, partner in spots:
        pl.semaphore_signal(barrier, inc=1, device_id=partner, device_id_type=MESH)

    def sending(level, chunk):
        first, count = CHUNKS[chunk]
        return pltpu.make_async_remote_copy(
            src_ref=own.at[level, pl.ds(first, count)],
            dst_ref=other.at[level, pl.ds(first, count)],
            send_sem=send_sem.at[level, chunk],
            recv_sem=recv_sem.at[level, chunk],
            device_id=spots[level][1],
            device_id_type=MESH,
        )

    for g in range(4):
        groups[g].wait()
        own[0, pl.ds(128 * g, 128), :] = c_in[:, pl.ds(128 * g, 128)].T
        if g == 0:
            pl.semaphore_wait(barrier, LEVELS)
        for chunk, (first, _) in enumerate(CHUNKS):
            if first // 128 == g:
                sending(0, chunk).start()

    for l in range(LEVELS):
        loads[l].wait()

        def prepare(block, carry):
            r = pl.multiple_of(128 * block, 128)
            for half in range(2):
                m = t_in[l, pl.ds(r, 128), pl.ds(RANK * half, RANK)].T
                h, w = split(m)
                high[l, half, :, pl.ds(r, 128)] = h
                low[l, half, :, pl.ds(r, 128)] = w
            return carry

        lax.fori_loop(0, 4, prepare, 0)

    for level, chunk in ORDER:
        first, count = CHUNKS[chunk]
        rows = pl.ds(first, count)
        upper = spots[level][0]
        total = product(own[level, rows, :], high.at[level, upper], low.at[level, upper])
        sending(level, chunk).wait_recv()
        total += product(other[level, rows, :], high.at[level, 1 - upper], low.at[level, 1 - upper])
        if level + 1 < LEVELS:
            own[level + 1, rows, :] = total
            sending(level + 1, chunk).start()
        else:
            last[rows, :] = total
            if (first + count) % 128 == 0:
                g = (first + count) // 128 - 1
                o_ref[:, pl.ds(128 * g, 128)] = last[pl.ds(128 * g, 128), :].T

    for level in range(LEVELS):
        for chunk in range(len(CHUNKS)):
            sending(level, chunk).wait_send()


def per_device(coeffs, transfer):
    count = len(CHUNKS)
    result = pl.pallas_call(
        kernel,
        out_shape=jax.ShapeDtypeStruct((RANK, RANK), F32),
        in_specs=[pl.BlockSpec(memory_space=pltpu.HBM)] * 2,
        out_specs=pl.BlockSpec(memory_space=pltpu.VMEM),
        scratch_shapes=[
            pltpu.VMEM((RANK, RANK), F32),
            pltpu.VMEM((LEVELS, RANK, 2 * RANK), F32),
            pltpu.VMEM((LEVELS, 2, RANK, RANK), BF16),
            pltpu.VMEM((LEVELS, 2, RANK, RANK), BF16),
            pltpu.VMEM((LEVELS, RANK, RANK), F32),
            pltpu.VMEM((LEVELS, RANK, RANK), F32),
            pltpu.VMEM((RANK, RANK), F32),
            pltpu.SemaphoreType.DMA((4,)),
            pltpu.SemaphoreType.DMA((LEVELS,)),
            pltpu.SemaphoreType.DMA((LEVELS, count)),
            pltpu.SemaphoreType.DMA((LEVELS, count)),
        ],
        compiler_params=pltpu.CompilerParams(collective_id=0, has_side_effects=True, vmem_limit_bytes=48 << 20),
        name="butterfly",
    )(pltpu.with_memory_space_constraint(coeffs[0], pltpu.HBM), transfer[:, 0])
    return result[None]


def solution(mesh):
    return jax.shard_map(
        per_device,
        mesh=mesh,
        in_specs=(P(AXES, None, None), P(None, AXES, None, None)),
        out_specs=P(AXES, None, None),
        check_vma=False,
    )
```

time: 128 us -> 67 us (0.52)
  waiting for transfers between devices: 88.2 us -> 0 us
  Pallas kernels: 0 us -> 65.9 us
  matrix products: 23.8 us -> 0 us
  starting transfers between devices: 12.1 us -> 0 us
  other arithmetic: 2.12 us -> 0 us
    ppermute x4 -> x0, waiting for transfers between devices: 88.2 us -> none  [from_partner(): return lax.ppermute(block, axis, route)]
    pallas_call x0 -> x1, Pallas kernels: none -> 65.9 us  [per_device(): pl.pallas_call(kernel, out_shape=jax.ShapeDtypeStruct((RANK, RANK), F32),...]
    dot_general x4 -> x0, matrix products: 23.8 us -> none  [apply_level(): jnp.dot(matrix, stacked, precision=lax.Precision.HIGHEST, preferred_eleme...]
    ppermute x4 -> x0, starting transfers between devices: 12.1 us -> none  [from_partner(): return lax.ppermute(block, axis, route)]
    select_n x4 -> x0, other arithmetic: 2.12 us -> none  [apply_level(): lower_part = jnp.where(upper == 1, other, own)]
    broadcast_in_dim x1 -> x0, local copies, waits for them, and re-layouts: 1.31 us -> none  [per_device(): return current[None]]
  transfers between devices with their start and end apart: 4 -> 0, of which waited for: 4 -> 0; matrix products, arithmetic and copies ran while one was open for 0% -> 0% of each run, Pallas kernels for 0% -> 0%
where the time goes in v1:
time: 67 us; the launch traced here: 66.9 us
  Pallas kernels  65.9 us (98%)
  local copies, waits for them, and re-layouts  0.97 us (1%)
    pallas_call x1, Pallas kernels, per_device(): pl.pallas_call(kernel, out_shape=jax.ShapeDtypeStruct((RANK, RANK), F32),...  65.9 us

profile of v1, /device:TPU:0, one launch (start us, length us, event | category | flops | bytes accessed | tf_op | source)
XLA Modules:
  0.0 66.9 jit_solution(6005747527533728351)
XLA Ops:
  0.0 65.9 %butterfly.1 = f32[512,512]{1,0:T(8,128)S(1)} custom-call(f32[512,512]{1,0:T(8,128)} %bitcast.5, f32[4,512,1024]{2,1,0:T(8,128)} %bitcast.4), custom_call_target="tpu_custom_call" | custom-call | tf_op jit(solution)/shard_map/butterfly/pallas_call | solution.py:115
  65.9 1.0 %copy.4 = f32[1,512,512]{2,1,0:T(8,128)} copy(f32[1,512,512]{2,1,0:T(8,128)S(1)} %bitcast.3) | data formatting | bytes 2097152

commit v2 on v1

--- a/solution.py
+++ b/solution.py
@@ -14,11 +14,19 @@
 F32 = jnp.float32
 AXES = ("gx", "gy", "gz")
 
-CHUNKS = tuple((64 * k, 64) for k in range(8))
+CHUNKS = (
+    (0, 16), (16, 16), (32, 32), (64, 32), (96, 32), (128, 32), (160, 32), (192, 32), (224, 32), (256, 32),
+    (288, 32), (320, 32), (352, 32), (384, 32), (416, 32), (448, 32), (480, 16), (496, 16),
+)
+PREPARE = -1
 ORDER = (
-    (0, 0), (0, 1), (0, 2), (1, 0), (0, 3), (1, 1), (0, 4), (1, 2), (2, 0), (0, 5), (0, 6), (1, 3), (2, 1), (3, 0),
-    (0, 7), (1, 4), (2, 2), (3, 1), (1, 5), (3, 2), (1, 6), (2, 3), (1, 7), (2, 4), (3, 3), (2, 5), (2, 6), (3, 4),
-    (2, 7), (3, 5), (3, 6), (3, 7),
+    (PREPARE, 1), (0, 0), (0, 1), (PREPARE, 2), (0, 2), (1, 0), (0, 3), (1, 1), (0, 4), (PREPARE, 3), (0, 5),
+    (1, 2), (2, 0), (0, 6), (1, 3), (2, 1), (0, 7), (1, 4), (0, 8), (3, 0), (1, 5), (0, 9), (2, 2), (0, 10),
+    (3, 1), (1, 6), (0, 11), (2, 3), (0, 12), (3, 2), (1, 7), (0, 13), (2, 4), (0, 14), (3, 3), (1, 8), (0,
+    15), (0, 16), (2, 5), (0, 17), (3, 4), (1, 9), (1, 10), (2, 6), (3, 5), (1, 11), (1, 12), (3, 6), (2, 7),
+    (1, 13), (1, 14), (2, 8), (3, 7), (1, 15), (1, 16), (1, 17), (3, 8), (2, 9), (2, 10), (2, 11), (2, 12),
+    (3, 9), (2, 13), (3, 10), (2, 14), (3, 11), (2, 15), (3, 12), (2, 16), (2, 17), (3, 13), (3, 14), (3, 15),
+    (3, 16), (3, 17),
 )
 
 
@@ -37,17 +45,15 @@
 
 def product(rows, high_ref, low_ref):
     high, low = split(rows)
-    m = high_ref[...]
-    total = jnp.dot(high, m, preferred_element_type=F32)
-    total += jnp.dot(low, m, preferred_element_type=F32)
-    total += jnp.dot(high, low_ref[...], preferred_element_type=F32)
-    return total
+    n = rows.shape[0]
+    both = jnp.dot(jnp.concatenate([high, low], axis=0), high_ref[...], preferred_element_type=F32)
+    return both[:n] + both[n:] + jnp.dot(high, low_ref[...], preferred_element_type=F32)
 
 
 def kernel(c_hbm, t_hbm, o_ref, c_in, t_in, high, low, own, other, last, c_sem, t_sem, send_sem, recv_sem):
     groups = [pltpu.make_async_copy(c_hbm.at[:, pl.ds(128 * g, 128)], c_in.at[:, pl.ds(128 * g, 128)], c_sem.at[g]) for g in range(4)]
     loads = [pltpu.make_async_copy(t_hbm.at[l], t_in.at[l], t_sem.at[l]) for l in range(LEVELS)]
-    for copy in groups + loads:
+    for copy in groups[:1] + loads[:1] + groups[1:] + loads[1:]:
         copy.start()
 
     spots = [position(l) for l in range(LEVELS)]
@@ -75,21 +81,25 @@
             if first // 128 == g:
                 sending(0, chunk).start()
 
-    for l in range(LEVELS):
-        loads[l].wait()
+    def prepare(level):
+        loads[level].wait()
 
-        def prepare(block, carry):
+        def step(block, carry):
             r = pl.multiple_of(128 * block, 128)
             for half in range(2):
-                m = t_in[l, pl.ds(r, 128), pl.ds(RANK * half, RANK)].T
+                m = t_in[level, pl.ds(r, 128), pl.ds(RANK * half, RANK)].T
                 h, w = split(m)
-                high[l, half, :, pl.ds(r, 128)] = h
-                low[l, half, :, pl.ds(r, 128)] = w
+                high[level, half, :, pl.ds(r, 128)] = h
+                low[level, half, :, pl.ds(r, 128)] = w
             return carry
 
-        lax.fori_loop(0, 4, prepare, 0)
+        lax.fori_loop(0, 4, step, 0)
 
+    prepare(0)
     for level, chunk in ORDER:
+        if level == PREPARE:
+            prepare(chunk)
+            continue
         first, count = CHUNKS[chunk]
         rows = pl.ds(first, count)
         upper = spots[level][0]

time: 67 us -> 67 us (level)
  no operation moved by 1% of the time
where the time goes in v2:
time: 67 us; the launch traced here: 66.9 us
  Pallas kernels  65.9 us (98%)
  local copies, waits for them, and re-layouts  0.97 us (1%)
    pallas_call x1, Pallas kernels, per_device(): pl.pallas_call(kernel, out_shape=jax.ShapeDtypeStruct((RANK, RANK), F32),...  65.9 us

profile of v2, /device:TPU:0, one launch (start us, length us, event | category | flops | bytes accessed | tf_op | source)
XLA Modules:
  0.0 66.9 jit_solution(17051257287436267693)
XLA Ops:
  0.0 65.9 %butterfly.1 = f32[512,512]{1,0:T(8,128)S(1)} custom-call(f32[512,512]{1,0:T(8,128)} %bitcast.5, f32[4,512,1024]{2,1,0:T(8,128)} %bitcast.4), custom_call_target="tpu_custom_call" | custom-call | tf_op jit(solution)/shard_map/butterfly/pallas_call | solution.py:125
  65.9 1.0 %copy.4 = f32[1,512,512]{2,1,0:T(8,128)} copy(f32[1,512,512]{2,1,0:T(8,128)S(1)} %bitcast.3) | data formatting | bytes 2097152

commit v3 on v2

--- a/solution.py
+++ b/solution.py
@@ -14,20 +14,15 @@
 F32 = jnp.float32
 AXES = ("gx", "gy", "gz")
 
-CHUNKS = (
-    (0, 16), (16, 16), (32, 32), (64, 32), (96, 32), (128, 32), (160, 32), (192, 32), (224, 32), (256, 32),
-    (288, 32), (320, 32), (352, 32), (384, 32), (416, 32), (448, 32), (480, 16), (496, 16),
-)
-PREPARE = -1
-ORDER = (
-    (PREPARE, 1), (0, 0), (0, 1), (PREPARE, 2), (0, 2), (1, 0), (0, 3), (1, 1), (0, 4), (PREPARE, 3), (0, 5),
-    (1, 2), (2, 0), (0, 6), (1, 3), (2, 1), (0, 7), (1, 4), (0, 8), (3, 0), (1, 5), (0, 9), (2, 2), (0, 10),
-    (3, 1), (1, 6), (0, 11), (2, 3), (0, 12), (3, 2), (1, 7), (0, 13), (2, 4), (0, 14), (3, 3), (1, 8), (0,
-    15), (0, 16), (2, 5), (0, 17), (3, 4), (1, 9), (1, 10), (2, 6), (3, 5), (1, 11), (1, 12), (3, 6), (2, 7),
-    (1, 13), (1, 14), (2, 8), (3, 7), (1, 15), (1, 16), (1, 17), (3, 8), (2, 9), (2, 10), (2, 11), (2, 12),
-    (3, 9), (2, 13), (3, 10), (2, 14), (3, 11), (2, 15), (3, 12), (2, 16), (2, 17), (3, 13), (3, 14), (3, 15),
-    (3, 16), (3, 17),
-)
+CHUNKS = tuple((32 * k, 32) for k in range(16))
+LAGS = (0, 3, 6, 9)
+
+
+def order():
+    for step in range(len(CHUNKS) + LAGS[-1]):
+        for level, lag in enumerate(LAGS):
+            if 0 <= step - lag < len(CHUNKS):
+                yield level, step - lag
 
 
 def position(level):
@@ -53,13 +48,14 @@
 def kernel(c_hbm, t_hbm, o_ref, c_in, t_in, high, low, own, other, last, c_sem, t_sem, send_sem, recv_sem):
     groups = [pltpu.make_async_copy(c_hbm.at[:, pl.ds(128 * g, 128)], c_in.at[:, pl.ds(128 * g, 128)], c_sem.at[g]) for g in range(4)]
     loads = [pltpu.make_async_copy(t_hbm.at[l], t_in.at[l], t_sem.at[l]) for l in range(LEVELS)]
-    for copy in groups[:1] + loads[:1] + groups[1:] + loads[1:]:
-        copy.start()
+    groups[0].start()
 
     spots = [position(l) for l in range(LEVELS)]
     barrier = pltpu.get_barrier_semaphore()
     for _, partner in spots:
         pl.semaphore_signal(barrier, inc=1, device_id=partner, device_id_type=MESH)
+    for copy in loads[:1] + groups[1:] + loads[1:]:
+        copy.start()
 
     def sending(level, chunk):
         first, count = CHUNKS[chunk]
@@ -96,10 +92,10 @@
         lax.fori_loop(0, 4, step, 0)
 
     prepare(0)
-    for level, chunk in ORDER:
-        if level == PREPARE:
+    prepare(1)
+    for level, chunk in order():
+        if (level, chunk) in ((0, 2), (0, 3)):
             prepare(chunk)
-            continue
         first, count = CHUNKS[chunk]
         rows = pl.ds(first, count)
         upper = spots[level][0]

time: 67 us -> 64.7 us (0.966)
  Pallas kernels: 65.9 us -> 63.6 us
    pallas_call x1, Pallas kernels: 65.9 us -> 63.6 us  [per_device(): pl.pallas_call(kernel, out_shape=jax.ShapeDtypeStruct((RANK, RANK), F32),...]
where the time goes in v3:
time: 64.7 us; the launch traced here: 64.6 us
  Pallas kernels  63.6 us (98%)
  local copies, waits for them, and re-layouts  0.97 us (1%)
    pallas_call x1, Pallas kernels, per_device(): pl.pallas_call(kernel, out_shape=jax.ShapeDtypeStruct((RANK, RANK), F32),...  63.6 us

profile of v3, /device:TPU:0, one launch (start us, length us, event | category | flops | bytes accessed | tf_op | source)
XLA Modules:
  0.0 64.6 jit_solution(5150434893493291129)
XLA Ops:
  0.0 63.6 %butterfly.1 = f32[512,512]{1,0:T(8,128)S(1)} custom-call(f32[512,512]{1,0:T(8,128)} %bitcast.5, f32[4,512,1024]{2,1,0:T(8,128)} %bitcast.4), custom_call_target="tpu_custom_call" | custom-call | tf_op jit(solution)/shard_map/butterfly/pallas_call | solution.py:121
  63.6 1.0 %copy.4 = f32[1,512,512]{2,1,0:T(8,128)} copy(f32[1,512,512]{2,1,0:T(8,128)S(1)} %bitcast.3) | data formatting | bytes 2097152

commit v4 on v3

--- a/solution.py
+++ b/solution.py
@@ -14,8 +14,8 @@
 F32 = jnp.float32
 AXES = ("gx", "gy", "gz")
 
-CHUNKS = tuple((32 * k, 32) for k in range(16))
-LAGS = (0, 3, 6, 9)
+CHUNKS = tuple((48 * k, min(48, 512 - 48 * k)) for k in range(11))
+LAGS = (0, 2, 4, 7)
 
 
 def order():
@@ -73,8 +73,8 @@
         own[0, pl.ds(128 * g, 128), :] = c_in[:, pl.ds(128 * g, 128)].T
         if g == 0:
             pl.semaphore_wait(barrier, LEVELS)
-        for chunk, (first, _) in enumerate(CHUNKS):
-            if first // 128 == g:
+        for chunk, (first, count) in enumerate(CHUNKS):
+            if (first + count - 1) // 128 == g:
                 sending(0, chunk).start()
 
     def prepare(level):
@@ -94,8 +94,8 @@
     prepare(0)
     prepare(1)
     for level, chunk in order():
-        if (level, chunk) in ((0, 2), (0, 3)):
-            prepare(chunk)
+        if (level, chunk) in ((0, 1), (0, 2)):
+            prepare(chunk + 1)
         first, count = CHUNKS[chunk]
         rows = pl.ds(first, count)
         upper = spots[level][0]
@@ -107,7 +107,7 @@
             sending(level + 1, chunk).start()
         else:
             last[rows, :] = total
-            if (first + count) % 128 == 0:
+            if (first + count) // 128 > first // 128:
                 g = (first + count) // 128 - 1
                 o_ref[:, pl.ds(128 * g, 128)] = last[pl.ds(128 * g, 128), :].T
 

time: 64.7 us -> 64.8 us (level)
  no operation moved by 1% of the time
where the time goes in v4:
time: 64.8 us; the launch traced here: 64.7 us
  Pallas kernels  63.7 us (98%)
  local copies, waits for them, and re-layouts  0.97 us (1%)
    pallas_call x1, Pallas kernels, per_device(): pl.pallas_call(kernel, out_shape=jax.ShapeDtypeStruct((RANK, RANK), F32),...  63.7 us

profile of v4, /device:TPU:0, one launch (start us, length us, event | category | flops | bytes accessed | tf_op | source)
XLA Modules:
  0.0 64.7 jit_solution(452961189505419803)
XLA Ops:
  0.0 63.7 %butterfly.1 = f32[512,512]{1,0:T(8,128)S(1)} custom-call(f32[512,512]{1,0:T(8,128)} %bitcast.5, f32[4,512,1024]{2,1,0:T(8,128)} %bitcast.4), custom_call_target="tpu_custom_call" | custom-call | tf_op jit(solution)/shard_map/butterfly/pallas_call | solution.py:121
  63.7 1.0 %copy.4 = f32[1,512,512]{2,1,0:T(8,128)} copy(f32[1,512,512]{2,1,0:T(8,128)S(1)} %bitcast.3) | data formatting | bytes 2097152

commit v5 on v4

--- a/solution.py
+++ b/solution.py
@@ -14,15 +14,20 @@
 F32 = jnp.float32
 AXES = ("gx", "gy", "gz")
 
-CHUNKS = tuple((48 * k, min(48, 512 - 48 * k)) for k in range(11))
+GROUPS = ((16, 32),) + 9 * ((48,),) + ((16, 16),)
+WIDTHS = sum(GROUPS, ())
+CHUNKS = tuple((sum(WIDTHS[:k]), WIDTHS[k]) for k in range(len(WIDTHS)))
 LAGS = (0, 2, 4, 7)
 
 
 def order():
-    for step in range(len(CHUNKS) + LAGS[-1]):
+    for step in range(len(GROUPS) + LAGS[-1]):
         for level, lag in enumerate(LAGS):
-            if 0 <= step - lag < len(CHUNKS):
-                yield level, step - lag
+            group = step - lag
+            if 0 <= group < len(GROUPS):
+                first = sum(map(len, GROUPS[:group]))
+                for chunk in range(first, first + len(GROUPS[group])):
+                    yield level, chunk, group
 
 
 def position(level):
@@ -93,9 +98,9 @@
 
     prepare(0)
     prepare(1)
-    for level, chunk in order():
-        if (level, chunk) in ((0, 1), (0, 2)):
-            prepare(chunk + 1)
+    for level, chunk, group in order():
+        if (level, group) in ((0, 1), (0, 2)):
+            prepare(group + 1)
         first, count = CHUNKS[chunk]
         rows = pl.ds(first, count)
         upper = spots[level][0]

time: 64.8 us -> 64.8 us (level)
  no operation moved by 1% of the time
where the time goes in v5:
time: 64.8 us; the launch traced here: 64.7 us
  Pallas kernels  63.7 us (98%)
  local copies, waits for them, and re-layouts  0.97 us (1%)
    pallas_call x1, Pallas kernels, per_device(): pl.pallas_call(kernel, out_shape=jax.ShapeDtypeStruct((RANK, RANK), F32),...  63.7 us

profile of v5, /device:TPU:0, one launch (start us, length us, event | category | flops | bytes accessed | tf_op | source)
XLA Modules:
  0.0 64.7 jit_solution(790729684852695232)
XLA Ops:
  0.0 63.7 %butterfly.1 = f32[512,512]{1,0:T(8,128)S(1)} custom-call(f32[512,512]{1,0:T(8,128)} %bitcast.5, f32[4,512,1024]{2,1,0:T(8,128)} %bitcast.4), custom_call_target="tpu_custom_call" | custom-call | tf_op jit(solution)/shard_map/butterfly/pallas_call | solution.py:126
  63.7 1.0 %copy.4 = f32[1,512,512]{2,1,0:T(8,128)} copy(f32[1,512,512]{2,1,0:T(8,128)S(1)} %bitcast.3) | data formatting | bytes 2097152

commit v6 on v4

--- a/solution.py
+++ b/solution.py
@@ -68,14 +68,19 @@
             device_id_type=MESH,
         )
 
+    core = lax.rem(lax.axis_index("gz"), 2)
+
+    def send_first(g):
+        for chunk, (first, count) in enumerate(CHUNKS):
+            if (first + count - 1) // 128 == g:
+                sending(0, chunk).start()
+
     for g in range(4):
         groups[g].wait()
         own[0, pl.ds(128 * g, 128), :] = c_in[:, pl.ds(128 * g, 128)].T
         if g == 0:
             pl.semaphore_wait(barrier, LEVELS)
-        for chunk, (first, count) in enumerate(CHUNKS):
-            if (first + count - 1) // 128 == g:
-                sending(0, chunk).start()
+        pl.when(core == 0)(functools.partial(send_first, g))
 
     def prepare(level):
         loads[level].wait()
@@ -92,6 +97,12 @@
         lax.fori_loop(0, 4, step, 0)
 
     prepare(0)
+
+    @pl.when(core == 1)
+    def _():
+        for g in range(4):
+            send_first(g)
+
     prepare(1)
     for level, chunk in order():
         if (level, chunk) in ((0, 1), (0, 2)):

time: 64.8 us -> 67.1 us (1.035); the launches traced: 64.7 us -> 65.8 us
  Pallas kernels: 63.7 us -> 64.8 us
    pallas_call x1, Pallas kernels: 63.7 us -> 64.8 us  [per_device(): pl.pallas_call(kernel, out_shape=jax.ShapeDtypeStruct((RANK, RANK), F32),...]
where the time goes in v6:
time: 67.1 us; the launch traced here: 65.8 us
  Pallas kernels  64.8 us (97%)
  local copies, waits for them, and re-layouts  0.97 us (1%)
    pallas_call x1, Pallas kernels, per_device(): pl.pallas_call(kernel, out_shape=jax.ShapeDtypeStruct((RANK, RANK), F32),...  64.8 us

profile of v6, /device:TPU:0, one launch (start us, length us, event | category | flops | bytes accessed | tf_op | source)
XLA Modules:
  0.0 65.8 jit_solution(17811612738948414474)
XLA Ops:
  0.0 64.8 %butterfly.1 = f32[512,512]{1,0:T(8,128)S(1)} custom-call(f32[512,512]{1,0:T(8,128)} %bitcast.5, f32[4,512,1024]{2,1,0:T(8,128)} %bitcast.4), custom_call_target="tpu_custom_call" | custom-call | tf_op jit(solution)/shard_map/butterfly/pallas_call | solution.py:132
  64.8 1.0 %copy.4 = f32[1,512,512]{2,1,0:T(8,128)} copy(f32[1,512,512]{2,1,0:T(8,128)S(1)} %bitcast.3) | data formatting | bytes 2097152

commit v7 on v4

--- a/solution.py
+++ b/solution.py
@@ -116,6 +116,14 @@
             sending(level, chunk).wait_send()
 
 
+def write_out(in_ref, o_hbm, sem):
+    copies = [pltpu.make_async_copy(in_ref.at[pl.ds(64 * i, 64)], o_hbm.at[pl.ds(64 * i, 64)], sem.at[i]) for i in range(8)]
+    for copy in copies:
+        copy.start()
+    for copy in copies:
+        copy.wait()
+
+
 def per_device(coeffs, transfer):
     count = len(CHUNKS)
     result = pl.pallas_call(
@@ -139,7 +147,15 @@
         compiler_params=pltpu.CompilerParams(collective_id=0, has_side_effects=True, vmem_limit_bytes=48 << 20),
         name="butterfly",
     )(pltpu.with_memory_space_constraint(coeffs[0], pltpu.HBM), transfer[:, 0])
-    return result[None]
+    return pl.pallas_call(
+        write_out,
+        out_shape=jax.ShapeDtypeStruct((RANK, RANK), F32),
+        in_specs=[pl.BlockSpec(memory_space=pltpu.VMEM)],
+        out_specs=pl.BlockSpec(memory_space=pltpu.HBM),
+        scratch_shapes=[pltpu.SemaphoreType.DMA((8,))],
+        compiler_params=pltpu.CompilerParams(vmem_limit_bytes=4 << 20),
+        name="write_out",
+    )(result)[None]
 
 
 def solution(mesh):

time: 64.8 us -> 64.8 us (level)
  Pallas kernels: 63.7 us -> 64.7 us
  local copies, waits for them, and re-layouts: 0.97 us -> 0 us
    pallas_call x0 -> x1, Pallas kernels: none -> 1.03 us  [per_device(): pl.pallas_call(write_out, out_shape=jax.ShapeDtypeStruct((RANK, RANK), F3...]
    unnamed x1 -> x0, local copies, waits for them, and re-layouts: 0.97 us -> none
where the time goes in v7:
time: 64.8 us; the launch traced here: 64.7 us
  Pallas kernels  64.7 us (100%)
    pallas_call x1, Pallas kernels, per_device(): pl.pallas_call(kernel, out_shape=jax.ShapeDtypeStruct((RANK, RANK), F32),...  63.7 us

profile of v7, /device:TPU:0, one launch (start us, length us, event | category | flops | bytes accessed | tf_op | source)
XLA Modules:
  0.0 64.7 jit_solution(14343970537537480734)
XLA Ops:
  0.0 63.7 %butterfly.1.in_ref = f32[512,512]{1,0:T(8,128)S(1)} custom-call(f32[512,512]{1,0:T(8,128)} %bitcast.4, f32[4,512,1024]{2,1,0:T(8,128)} %bitcast.3), custom_call_target="tpu_custom_call" | custom-call | tf_op jit(solution)/shard_map/butterfly/pallas_call | solution.py:129
  63.7 1.0 %write_out.1 = f32[512,512]{1,0:T(8,128)} custom-call(f32[512,512]{1,0:T(8,128)S(1)} %butterfly.1.in_ref), custom_call_target="tpu_custom_call" | custom-call | tf_op jit(solution)/shard_map/write_out/pallas_call | solution.py:150

commit v8 on v4

--- a/solution.py
+++ b/solution.py
@@ -15,7 +15,7 @@
 AXES = ("gx", "gy", "gz")
 
 CHUNKS = tuple((48 * k, min(48, 512 - 48 * k)) for k in range(11))
-LAGS = (0, 2, 4, 7)
+LAGS = (0, 2, 4, 8)
 
 
 def order():

time: 64.8 us -> 64.8 us (level)
  no operation moved by 1% of the time
where the time goes in v8:
time: 64.8 us; the launch traced here: 64.7 us
  Pallas kernels  63.7 us (98%)
  local copies, waits for them, and re-layouts  0.97 us (1%)
    pallas_call x1, Pallas kernels, per_device(): pl.pallas_call(kernel, out_shape=jax.ShapeDtypeStruct((RANK, RANK), F32),...  63.7 us

profile of v8, /device:TPU:0, one launch (start us, length us, event | category | flops | bytes accessed | tf_op | source)
XLA Modules:
  0.0 64.7 jit_solution(6092100172488535722)
XLA Ops:
  0.0 63.7 %butterfly.1 = f32[512,512]{1,0:T(8,128)S(1)} custom-call(f32[512,512]{1,0:T(8,128)} %bitcast.5, f32[4,512,1024]{2,1,0:T(8,128)} %bitcast.4), custom_call_target="tpu_custom_call" | custom-call | tf_op jit(solution)/shard_map/butterfly/pallas_call | solution.py:121
  63.7 1.0 %copy.4 = f32[1,512,512]{2,1,0:T(8,128)} copy(f32[1,512,512]{2,1,0:T(8,128)S(1)} %bitcast.3) | data formatting | bytes 2097152
